TPU v7x, 128 devices: a whole 4x4x4 slice. The times are simulated.
128 devices in a mesh: fsdp: 32 (over z_lo, x, y), dp: 4 (over z_hi, core).
Axes of the slice: x: 4, y: 4, z: 4 (z_hi: 2, z_lo: 2; z = z_hi * 2 + z_lo), core: 2. Of those that a mesh axis runs over, the one named last changes fastest.
Arguments:
- teacher_hidden: bfloat16 [1024, 8192], P(('fsdp', 'dp'))
- student_hidden: bfloat16 [1024, 4096], P(('fsdp', 'dp'))
- teacher_head: bfloat16 [8192, 65536], P('dp', 'fsdp'), may hold values from -0.1875 to 0.1875
- student_head: bfloat16 [4096, 65536], P('dp', 'fsdp'), may hold values from -0.25 to 0.25
- actions: int32 [1024], replicated, may hold values from 0 to 65535
- advantages: float32 [1024], replicated, may hold values from -0.21875 to 0.21875
- loss_mask: int32 [1024], replicated, may hold values 0 or 1
Outputs:
- token_loss: float32 [1024], P('dp')
- head_grad: float32 [4096, 65536], P('dp', 'fsdp')
- hidden_grad: bfloat16 [1024, 4096], P('fsdp', 'dp')
All inputs are finite; a program needn't handle non-finite values.
Results may differ from a plain program's by a relative error of at most 0.0048.
Values may be sent and summed in bfloat16 or wider, within the bound.
No kernel may reach another device: no remote copies, remote signals or barrier semaphores. Data moves between devices by JAX's collectives and lax.ppermute only.
A program may use at most 128 MiB of HBM per device.

v0:
```python
import jax
import jax.numpy as jnp
from jax import lax
from jax.sharding import PartitionSpec as P

kl_weight = 0.5


def shards(
    teacher_hidden, student_hidden, teacher_head, student_head, actions, advantages, loss_mask
):
    teacher_part, student_part = (
        lax.all_to_all(teacher_hidden, "dp", split_axis=1, concat_axis=0, tiled=True),
        lax.all_to_all(student_hidden, "dp", split_axis=1, concat_axis=0, tiled=True),
    )
    teacher_rows, student_rows = (
        lax.all_gather(teacher_part, "fsdp", axis=0, tiled=True),
        lax.all_gather(student_part, "fsdp", axis=0, tiled=True),
    )
    total_rows = teacher_rows.shape[0]
    share = total_rows // lax.axis_size("dp")
    teacher_partial = jnp.dot(teacher_rows, teacher_head, preferred_element_type=jnp.float32)
    student_partial = jnp.dot(student_rows, student_head, preferred_element_type=jnp.float32)
    teacher_logits, student_logits = (
        lax.psum_scatter(teacher_partial, "dp", scatter_dimension=0, tiled=True),
        lax.psum_scatter(student_partial, "dp", scatter_dimension=0, tiled=True),
    )
    first_row = lax.axis_index("dp") * share
    chosen = lax.dynamic_slice_in_dim(actions, first_row, share)
    benefit = lax.dynamic_slice_in_dim(advantages, first_row, share)
    weight = lax.dynamic_slice_in_dim(loss_mask, first_row, share).astype(jnp.float32)
    vocab_shard = teacher_logits.shape[1]
    columns = lax.axis_index("fsdp") * vocab_shard + jnp.arange(vocab_shard, dtype=jnp.int32)
    onehot = (chosen[:, None] == columns[None, :]).astype(jnp.float32)
    local_pick = jnp.sum(onehot * student_logits, axis=1)
    teacher_max, student_max = lax.pmax(
        (jnp.max(teacher_logits, axis=1), jnp.max(student_logits, axis=1)), "fsdp"
    )
    teacher_exp = jnp.exp(teacher_logits - teacher_max[:, None])
    student_exp = jnp.exp(student_logits - student_max[:, None])
    teacher_sum, student_sum, cross, pick = lax.psum(
        (
            jnp.sum(teacher_exp, axis=1),
            jnp.sum(student_exp, axis=1),
            jnp.sum(teacher_exp * (teacher_logits - student_logits), axis=1),
            local_pick,
        ),
        "fsdp",
    )
    teacher_lse = teacher_max + jnp.log(teacher_sum)
    student_lse = student_max + jnp.log(student_sum)
    kl = cross / teacher_sum - teacher_lse + student_lse
    action_logp = pick - student_lse
    losses = weight * (kl_weight * kl - benefit * action_logp)
    teacher_prob = teacher_exp / teacher_sum[:, None]
    student_prob = student_exp / student_sum[:, None]
    logit_grad = (
        weight[:, None]
        * (kl_weight * (student_prob - teacher_prob) + benefit[:, None] * (student_prob - onehot))
    ).astype(jnp.bfloat16)
    grad_all = lax.all_gather(logit_grad, "dp", axis=0, tiled=True)
    head_grad = lax.dot_general(
        student_rows, grad_all, (((0,), (0,)), ((), ())), preferred_element_type=jnp.float32
    )
    hidden_grad = lax.psum_scatter(
        lax.dot_general(
            grad_all, student_head, (((1,), (1,)), ((), ())), preferred_element_type=jnp.float32
        ),
        "fsdp",
        scatter_dimension=0,
        tiled=True,
    ).astype(jnp.bfloat16)
    return (losses, head_grad, hidden_grad)


def solution(mesh):
    placed = (
        P(("fsdp", "dp"), None),
        P(("fsdp", "dp"), None),
        P("dp", "fsdp"),
        P("dp", "fsdp"),
        P(),
        P(),
        P(),
    )
    return jax.shard_map(
        shards,
        mesh=mesh,
        in_specs=placed,
        out_specs=(P("dp"), P("dp", "fsdp"), P("fsdp", "dp")),
        check_vma=False,
    )
```

profile of v0, /device:TPU:0, one launch (start us, length us, event | category | flops | bytes accessed | tf_op | source)
XLA Modules:
  0.0 882.2 jit_solution(9315248481486084040)
XLA Ops:
  7.2 0.0 all-gather.6.cloned.1.call-start
  7.2 11.0 %all_to_all.38 = bf16[8,4,1024]{2,0,1:T(8,128)(2,1)} all-to-all(bf16[8,4,1024]{2,0,1:T(8,128)(2,1)} %bitcast.21), channel_id=1, replica_groups=mesh['fsdp'=32,'dp'=4] {'dp'}, dimensions={1} | all-to-all | bytes 131072 | tf_op jit(solution)/shard_map/all_to_all | solution.py:14
  18.2 0.0 all-gather.6.cloned.1.call-update
  18.2 0.0 all-gather.4.cloned.1.call-start
  18.3 10.1 %all_to_all.39 = bf16[8,4,2048]{2,0,1:T(8,128)(2,1)} all-to-all(bf16[8,4,2048]{2,0,1:T(8,128)(2,1)} %bitcast.20), channel_id=1, replica_groups=mesh['fsdp'=32,'dp'=4] {'dp'}, dimensions={1} | all-to-all | bytes 262144 | tf_op jit(solution)/shard_map/all_to_all | solution.py:13
  28.4 0.0 all-gather.4.cloned.1.call-update
  28.4 0.0 reduce-scatter.6.cloned.1.call-start
  28.5 141.8 %all-gather.6.cloned.1.call-done = bf16[1024,1024]{1,0:T(8,128)(2,1)} async-done(((bf16[32,1024]{1,0:T(8,128)(2,1)}), bf16[1024,1024]{1,0:T(8,128)(2,1)}) %all-gather.6.cloned.1.call-update) | async-done | bytes 2097168 | tf_op jit(solution)/shard_map/all_gather | solution.py:18
  170.3 10.5 %fusion.9 = f32[1024,2048]{1,0:T(8,128)} fusion(bf16[1024,1024]{1,0:T(8,128)(2,1)} %all-gather.6.cloned.1.call-done, bf16[1024,2048]{1,0:T(8,128)(2,1)} %param.10), kind=kOutput, calls=%fused_computation.18 | convolution fusion | flops 4294967296 | bytes 14680064 | tf_op jit(solution)/shard_map/dot_general | solution.py:23
  180.8 0.0 reduce-scatter.6.cloned.1.call-update
  180.8 0.0 reduce-scatter.4.cloned.1.call-start
  180.9 147.8 %all-gather.4.cloned.1.call-done = bf16[1024,2048]{1,0:T(8,128)(2,1)} async-done(((bf16[32,2048]{1,0:T(8,128)(2,1)}), bf16[1024,2048]{1,0:T(8,128)(2,1)}) %all-gather.4.cloned.1.call-update) | async-done | bytes 4194320 | tf_op jit(solution)/shard_map/all_gather | solution.py:17
  328.7 14.8 %fusion.8 = f32[1024,2048]{1,0:T(8,128)} fusion(bf16[1024,2048]{1,0:T(8,128)(2,1)} %all-gather.4.cloned.1.call-done, bf16[2048,2048]{1,0:T(8,128)(2,1)} %param.9), kind=kOutput, calls=%fused_computation.17 | convolution fusion | flops 8589934592 | bytes 20971520 | tf_op jit(solution)/shard_map/dot_general | solution.py:22
  343.4 0.0 reduce-scatter.4.cloned.1.call-update
  343.4 0.0 all-gather.8.cloned.1.call-start
  343.5 0.8 dynamic_slice.11
  344.3 66.0 %reduce-scatter.6.cloned.1.call-done = f32[256,2048]{1,0:T(8,128)} async-done(((f32[1024,2048]{1,0:T(8,128)}), f32[256,2048]{1,0:T(8,128)}) %reduce-scatter.6.cloned.1.call-update) | async-done | bytes 2097168 | tf_op jit(solution)/shard_map/reduce_scatter | solution.py:26
  410.3 0.0 copy-start
  410.3 1.9 reduce_max.19
  412.2 78.9 %reduce-scatter.4.cloned.1.call-done = f32[256,2048]{1,0:T(8,128)} async-done(((f32[1024,2048]{1,0:T(8,128)}), f32[256,2048]{1,0:T(8,128)}) %reduce-scatter.4.cloned.1.call-update) | async-done | bytes 2097168 | tf_op jit(solution)/shard_map/reduce_scatter | solution.py:25
  491.1 1.8 reduce_max.18
  492.9 81.8 %all-reduce.1 = (f32[256]{0:T(256)S(1)}, f32[256]{0:T(256)S(1)}) all-reduce(f32[256]{0:T(256)S(1)} %reduce_max.18, f32[256]{0:T(256)S(1)} %reduce_max.19), channel_id=1, replica_groups=mesh['fsdp'=32,'dp'=4] {'fsdp'}, use_global_device_ids=true, to_apply=%region_2.0 | all-reduce | flops 512 | bytes 4096 | tf_op jit(solution)/shard_map/pmax | solution.py:36
  574.6 0.0 copy-done
  574.7 2.8 multiply_reduce_fusion
  577.5 76.8 %all-reduce = (f32[256]{0:T(256)S(1)}, f32[256]{0:T(256)S(1)}, f32[256]{0:T(256)S(1)}, f32[256]{0:T(256)S(1)}) all-reduce(f32[256]{0:T(256)S(1)} %get-tuple-element.8, f32[256]{0:T(256)S(1)} %get-tuple-element.9, f32[256]{0:T(256)S(1)} %get-tuple-element.7, f32[256]{0:T(256)S(1)} %get-tuple-element.6), channel_id=1, replica_groups=mesh['fsdp'=32,'dp'=4] {'fsdp'}, use_global_device_ids=true, to_apply=%region_13.0 | all-reduce | flops 1024 | bytes 8192 | tf_op jit(solution)/shard_map/psum | solution.py:41
  654.3 1.3 subtract_multiply_fusion
  655.7 3.4 fusion.5
  659.1 0.0 all-gather.8.cloned.1.call-update
  659.1 0.2 reduce-scatter.8.cloned.1.call-start
  659.4 35.1 %all-gather.8.cloned.1.call-done = bf16[1024,2048]{1,0:T(8,128)(2,1)} async-done(((bf16[256,2048]{1,0:T(8,128)(2,1)}), bf16[1024,2048]{1,0:T(8,128)(2,1)}) %all-gather.8.cloned.1.call-update) | async-done | bytes 4194320 | tf_op jit(solution)/shard_map/all_gather | solution.py:61
  694.5 10.0 %fusion.10 = f32[1024,1024]{1,0:T(8,128)} fusion(bf16[1024,2048]{1,0:T(8,128)(2,1)} %all-gather.8.cloned.1.call-done, bf16[1024,2048]{1,0:T(8,128)(2,1)} %param.10), kind=kOutput, calls=%fused_computation.19 | convolution fusion | flops 4294967296 | bytes 12582912 | tf_op jit(solution)/shard_map/dot_general | solution.py:66
  704.5 0.0 copy-start.1
  704.5 0.0 reduce-scatter.8.cloned.1.call-update
  704.5 1.6 copy-done.1
  706.1 9.0 %convolution_bitcast_fusion = f32[1024,2048]{0,1:T(8,128)} fusion(bf16[1024,2048]{1,0:T(8,128)(2,1)} %all-gather.8.cloned.1.call-done, bf16[1024,1024]{1,0:T(8,128)(2,1)S(1)} %copy-done.1), kind=kOutput, calls=%fused_computation | convolution fusion | flops 4294967296 | bytes 14680064 | tf_op jit(solution)/shard_map/dot_general | solution.py:62
  715.1 9.1 %copy.10 = f32[1024,2048]{1,0:T(8,128)} copy(f32[1024,2048]{0,1:T(8,128)} %convolution_bitcast_fusion) | data formatting | bytes 16777216
  724.2 149.6 %reduce-scatter.8.cloned.1.call-done = f32[32,1024]{1,0:T(8,128)} async-done(((f32[1024,1024]{1,0:T(8,128)}), f32[32,1024]{1,0:T(8,128)}) %reduce-scatter.8.cloned.1.call-update) | async-done | bytes 131088 | tf_op jit(solution)/shard_map/reduce_scatter | solution.py:65
  873.8 1.5 convert_element_type.15
  (1 shorter events, 0.0 us)
Async XLA Ops:
  7.2 163.1 %all-gather.6.cloned.1.call-start = ((), (), s32[]{:S(2)}) async-start(), calls=%async_computation.7 | async-start | bytes 2162688 | tf_op jit(solution)/shard_map/all_gather | solution.py:18
  18.2 310.4 %all-gather.4.cloned.1.call-start = ((), (), s32[]{:S(2)}) async-start(), calls=%async_computation.5 | async-start | bytes 4325376 | tf_op jit(solution)/shard_map/all_gather | solution.py:17
  28.4 381.9 %reduce-scatter.6.cloned.1.call-start = ((), (), s32[]{:S(2)}) async-start(), calls=%async_computation.8 | async-start | bytes 10485760 | tf_op jit(solution)/shard_map/reduce_scatter | solution.py:26
  180.8 310.3 %reduce-scatter.4.cloned.1.call-start = ((), (), s32[]{:S(2)}) async-start(), calls=%async_computation.6 | async-start | bytes 10485760 | tf_op jit(solution)/shard_map/reduce_scatter | solution.py:25
  343.4 351.1 %all-gather.8.cloned.1.call-start = ((), (), s32[]{:S(2)}) async-start(), calls=%async_computation.9 | async-start | bytes 5242880 | tf_op jit(solution)/shard_map/all_gather | solution.py:61
  410.3 164.4 %copy-start = (f32[256,2048]{1,0:T(8,128)S(1)}, f32[256,2048]{1,0:T(8,128)}, u32[]{:S(2)}) copy-start(f32[256,2048]{1,0:T(8,128)} %reduce-scatter.6.cloned.1.call-done) | copy-start | bytes 6291460
  659.1 214.7 %reduce-scatter.8.cloned.1.call-start = ((), (), s32[]{:S(2)}) async-start(), calls=%async_computation.10 | async-start | bytes 4325376 | tf_op jit(solution)/shard_map/reduce_scatter | solution.py:65
  704.5 1.6 copy-start.1
Sparse Core Ops, SparseCore 0:
  18.4 151.8 all-gather.5
  171.9 156.6 all-gather.3
  331.3 78.8 reduce-scatter.5
  413.4 77.6 reduce-scatter.3
  659.3 35.1 all-gather.7
  704.6 169.1 reduce-scatter.7
where the time goes:
time: 883 us; the launch traced here: 882 us
  waiting for transfers between devices  619 us (70%)
  blocking collectives  180 us (20%)
  matrix products  44.3 us (5%)
  between operations  14.1 us (2%)
  other arithmetic  12.9 us (1%)
  local copies, waits for them, and re-layouts  11.5 us (1%)
    reduce_scatter x1, waiting for transfers between devices, shards(): lax.psum_scatter(lax.dot_general(grad_all, student_head, (((1,), (1,)), (...  150 us
    all_gather x1, waiting for transfers between devices, shards(): lax.all_gather(teacher_part, 'fsdp', axis=0, tiled=True)  148 us
    all_gather x1, waiting for transfers between devices, shards(): lax.all_gather(student_part, 'fsdp', axis=0, tiled=True)  142 us
    pmax x1, blocking collectives, shards(): lax.pmax((jnp.max(teacher_logits, axis=1), jnp.max(student_logits, axis=1...  81.8 us
    reduce_scatter x1, waiting for transfers between devices, shards(): lax.psum_scatter(teacher_partial, 'dp', scatter_dimension=0, tiled=True)  78.9 us
    psum x1, blocking collectives, shards(): lax.psum((jnp.sum(teacher_exp, axis=1), jnp.sum(student_exp, axis=1), jnp...  76.8 us
    reduce_scatter x1, waiting for transfers between devices, shards(): lax.psum_scatter(student_partial, 'dp', scatter_dimension=0, tiled=True)  66 us
    all_gather x1, waiting for transfers between devices, shards(): grad_all = lax.all_gather(logit_grad, 'dp', axis=0, tiled=True)  35.1 us
  transfers between devices with their start and end apart: 6, of which 6 were waited for; matrix products, arithmetic and copies ran while one was open for 5% of the time, Pallas kernels for 0%

commit v1 on v0

--- a/solution.py
+++ b/solution.py
@@ -15,7 +15,9 @@
     )
     teacher_rows, student_rows = (
         lax.all_gather(teacher_part, "fsdp", axis=0, tiled=True),
-        lax.all_gather(student_part, "fsdp", axis=0, tiled=True),
+        jnp.concatenate(
+            lax.all_to_all(jnp.stack([student_part] * lax.axis_size("fsdp")), "fsdp", 0, 0), axis=0
+        ),
     )
     total_rows = teacher_rows.shape[0]
     share = total_rows // lax.axis_size("dp")

time: 883 us -> 674 us (0.76)
  waiting for transfers between devices: 619 us -> 371 us
  blocking collectives: 180 us -> 220 us
    all_gather x1 -> x0, waiting for transfers between devices: 142 us -> none  [shards(): lax.all_gather(student_part, 'fsdp', axis=0, tiled=True)]
    reduce_scatter x1, waiting for transfers between devices: 66 us -> 0.01 us  [shards(): lax.psum_scatter(student_partial, 'dp', scatter_dimension=0, tiled=True)]
    all_to_all x0 -> x1, blocking collectives: none -> 40.7 us  [shards(): lax.all_to_all(jnp.stack([student_part] * lax.axis_size('fsdp')), 'fsdp',...]
    all_gather x1, waiting for transfers between devices: 148 us -> 113 us  [shards(): lax.all_gather(teacher_part, 'fsdp', axis=0, tiled=True)]
  transfers between devices with their start and end apart: 6 -> 5, of which waited for: 6 -> 4; matrix products, arithmetic and copies ran while one was open for 5% -> 6% of each run, Pallas kernels for 0% -> 0%
where the time goes in v1:
time: 674 us; the launch traced here: 673 us
  waiting for transfers between devices  371 us (55%)
  blocking collectives  220 us (33%)
  matrix products  40.1 us (6%)
  between operations  15.7 us (2%)
  local copies, waits for them, and re-layouts  13.1 us (2%)
  other arithmetic  12.9 us (2%)
    reduce_scatter x1, waiting for transfers between devices, shards(): lax.psum_scatter(lax.dot_general(grad_all, student_head, (((1,), (1,)), (...  149 us
    all_gather x1, waiting for transfers between devices, shards(): lax.all_gather(teacher_part, 'fsdp', axis=0, tiled=True)  113 us
    pmax x1, blocking collectives, shards(): lax.pmax((jnp.max(teacher_logits, axis=1), jnp.max(student_logits, axis=1...  81.8 us
    psum x1, blocking collectives, shards(): lax.psum((jnp.sum(teacher_exp, axis=1), jnp.sum(student_exp, axis=1), jnp...  76.8 us
    reduce_scatter x1, waiting for transfers between devices, shards(): lax.psum_scatter(teacher_partial, 'dp', scatter_dimension=0, tiled=True)  73.8 us
    all_to_all x1, blocking collectives, shards(): lax.all_to_all(jnp.stack([student_part] * lax.axis_size('fsdp')), 'fsdp',...  40.7 us
    all_gather x1, waiting for transfers between devices, shards(): grad_all = lax.all_gather(logit_grad, 'dp', axis=0, tiled=True)  35 us
    dot_general x1, matrix products, shards(): jnp.dot(teacher_rows, teacher_head, preferred_element_type=jnp.float32)  14.5 us
  transfers between devices with their start and end apart: 5, of which 4 were waited for; matrix products, arithmetic and copies ran while one was open for 6% of the time, Pallas kernels for 0%

profile of v1, /device:TPU:0, one launch (start us, length us, event | category | flops | bytes accessed | tf_op | source)
XLA Modules:
  0.0 673.0 jit_solution(659979728416328940)
XLA Ops:
  8.0 0.0 all-gather.3.cloned.1.call-start
  8.0 11.5 %all_to_all.40 = bf16[8,4,2048]{2,0,1:T(8,128)(2,1)} all-to-all(bf16[8,4,2048]{2,0,1:T(8,128)(2,1)} %bitcast.23), channel_id=1, replica_groups=mesh['fsdp'=32,'dp'=4] {'dp'}, dimensions={1} | all-to-all | bytes 262144 | tf_op jit(solution)/shard_map/all_to_all | solution.py:13
  19.5 0.0 all-gather.3.cloned.1.call-update
  19.5 0.0 reduce-scatter.6.cloned.1.call-start
  19.6 8.9 %all_to_all.41 = bf16[8,4,1024]{2,0,1:T(8,128)(2,1)S(1)} all-to-all(bf16[8,4,1024]{2,0,1:T(8,128)(2,1)} %bitcast.24), channel_id=1, replica_groups=mesh['fsdp'=32,'dp'=4] {'dp'}, dimensions={1} | all-to-all | bytes 131072 | tf_op jit(solution)/shard_map/all_to_all | solution.py:14
  28.5 0.2 stack.5
  28.7 0.0 copy-start.3
  28.8 40.7 %all_to_all.42 = bf16[32,32,1024]{2,1,0:T(8,128)(2,1)S(1)} all-to-all(bf16[32,32,1024]{2,1,0:T(8,128)(2,1)S(1)} %stack.5), channel_id=1, replica_groups=mesh['fsdp'=32,'dp'=4] {'fsdp'}, dimensions={0} | all-to-all | bytes 4194304 | tf_op jit(solution)/shard_map/all_to_all | solution.py:19
  69.5 0.0 copy-start.1
  69.5 1.3 copy-done.1
  70.8 0.0 copy-done.3
  70.8 6.6 fusion.9
  77.5 0.0 reduce-scatter.6.cloned.1.call-update
  77.5 0.0 reduce-scatter.4.cloned.1.call-start
  77.5 113.4 %all-gather.3.cloned.1.call-done = bf16[1024,2048]{1,0:T(8,128)(2,1)} async-done(((bf16[32,2048]{1,0:T(8,128)(2,1)}), bf16[1024,2048]{1,0:T(8,128)(2,1)}) %all-gather.3.cloned.1.call-update) | async-done | bytes 4194320 | tf_op jit(solution)/shard_map/all_gather | solution.py:17
  190.9 14.5 %fusion.8 = f32[1024,2048]{1,0:T(8,128)} fusion(bf16[1024,2048]{1,0:T(8,128)(2,1)} %all-gather.3.cloned.1.call-done, bf16[2048,2048]{1,0:T(8,128)(2,1)} %param.9), kind=kOutput, calls=%fused_computation.17 | convolution fusion | flops 8589934592 | bytes 20971520 | tf_op jit(solution)/shard_map/dot_general | solution.py:24
  205.4 0.0 reduce-scatter.4.cloned.1.call-update
  205.4 0.0 all-gather.5.cloned.1.call-start
  205.5 0.8 dynamic_slice.11
  206.2 0.0 reduce-scatter.6.cloned.1.call-done
  206.2 0.0 copy-start
  206.3 1.9 reduce_max.19
  208.2 73.8 %reduce-scatter.4.cloned.1.call-done = f32[256,2048]{1,0:T(8,128)} async-done(((f32[1024,2048]{1,0:T(8,128)}), f32[256,2048]{1,0:T(8,128)}) %reduce-scatter.4.cloned.1.call-update) | async-done | bytes 2097168 | tf_op jit(solution)/shard_map/reduce_scatter | solution.py:27
  282.0 1.8 reduce_max.18
  283.7 81.8 %all-reduce.1 = (f32[256]{0:T(256)S(1)}, f32[256]{0:T(256)S(1)}) all-reduce(f32[256]{0:T(256)S(1)} %reduce_max.18, f32[256]{0:T(256)S(1)} %reduce_max.19), channel_id=1, replica_groups=mesh['fsdp'=32,'dp'=4] {'fsdp'}, use_global_device_ids=true, to_apply=%region_2.0 | all-reduce | flops 512 | bytes 4096 | tf_op jit(solution)/shard_map/pmax | solution.py:38
  365.5 0.0 copy-done
  365.5 2.8 multiply_reduce_fusion
  368.3 76.8 %all-reduce = (f32[256]{0:T(256)S(1)}, f32[256]{0:T(256)S(1)}, f32[256]{0:T(256)S(1)}, f32[256]{0:T(256)S(1)}) all-reduce(f32[256]{0:T(256)S(1)} %get-tuple-element.8, f32[256]{0:T(256)S(1)} %get-tuple-element.9, f32[256]{0:T(256)S(1)} %get-tuple-element.7, f32[256]{0:T(256)S(1)} %get-tuple-element.6), channel_id=1, replica_groups=mesh['fsdp'=32,'dp'=4] {'fsdp'}, use_global_device_ids=true, to_apply=%region_13.0 | all-reduce | flops 1024 | bytes 8192 | tf_op jit(solution)/shard_map/psum | solution.py:43
  445.2 1.3 subtract_multiply_fusion
  446.5 3.4 fusion.5
  450.0 0.0 all-gather.5.cloned.1.call-update
  450.0 0.2 reduce-scatter.8.cloned.1.call-start
  450.2 35.0 %all-gather.5.cloned.1.call-done = bf16[1024,2048]{1,0:T(8,128)(2,1)} async-done(((bf16[256,2048]{1,0:T(8,128)(2,1)}), bf16[1024,2048]{1,0:T(8,128)(2,1)}) %all-gather.5.cloned.1.call-update) | async-done | bytes 4194320 | tf_op jit(solution)/shard_map/all_gather | solution.py:63
  485.2 10.0 %fusion.10 = f32[1024,1024]{1,0:T(8,128)} fusion(bf16[1024,2048]{1,0:T(8,128)(2,1)} %all-gather.5.cloned.1.call-done, bf16[1024,2048]{1,0:T(8,128)(2,1)} %param.10), kind=kOutput, calls=%fused_computation.19 | convolution fusion | flops 4294967296 | bytes 12582912 | tf_op jit(solution)/shard_map/dot_general | solution.py:68
  495.2 0.0 copy-start.2
  495.2 0.0 reduce-scatter.8.cloned.1.call-update
  495.2 1.6 copy-done.2
  496.7 9.0 %convolution_bitcast_fusion = f32[1024,2048]{0,1:T(8,128)} fusion(bf16[1024,2048]{1,0:T(8,128)(2,1)} %all-gather.5.cloned.1.call-done, bf16[1024,1024]{1,0:T(8,128)(2,1)S(1)} %bitcast.20), kind=kOutput, calls=%fused_computation | convolution fusion | flops 4294967296 | bytes 14680064 | tf_op jit(solution)/shard_map/dot_general | solution.py:64
  505.8 9.1 %copy.10 = f32[1024,2048]{1,0:T(8,128)} copy(f32[1024,2048]{0,1:T(8,128)} %convolution_bitcast_fusion) | data formatting | bytes 16777216
  514.9 149.0 %reduce-scatter.8.cloned.1.call-done = f32[32,1024]{1,0:T(8,128)} async-done(((f32[1024,1024]{1,0:T(8,128)}), f32[32,1024]{1,0:T(8,128)}) %reduce-scatter.8.cloned.1.call-update) | async-done | bytes 131088 | tf_op jit(solution)/shard_map/reduce_scatter | solution.py:67
  663.9 1.5 convert_element_type.15
  (1 shorter events, 0.0 us)
Async XLA Ops:
  8.0 182.9 %all-gather.3.cloned.1.call-start = ((), (), s32[]{:S(2)}) async-start(), calls=%async_computation.6 | async-start | bytes 4325376 | tf_op jit(solution)/shard_map/all_gather | solution.py:17
  19.5 186.7 %reduce-scatter.6.cloned.1.call-start = ((), (), s32[]{:S(2)}) async-start(), calls=%async_computation.8 | async-start | bytes 10485760 | tf_op jit(solution)/shard_map/reduce_scatter | solution.py:28
  28.7 42.1 %copy-start.3 = (bf16[1024,2048]{1,0:T(8,128)(2,1)S(1)}, bf16[1024,2048]{1,0:T(8,128)(2,1)}, u32[]{:S(2)}) copy-start(bf16[1024,2048]{1,0:T(8,128)(2,1)} %param.10) | copy-start | bytes 12582916
  69.5 1.4 copy-start.1
  77.5 204.5 %reduce-scatter.4.cloned.1.call-start = ((), (), s32[]{:S(2)}) async-start(), calls=%async_computation.7 | async-start | bytes 10485760 | tf_op jit(solution)/shard_map/reduce_scatter | solution.py:27
  205.4 279.8 %all-gather.5.cloned.1.call-start = ((), (), s32[]{:S(2)}) async-start(), calls=%async_computation.9 | async-start | bytes 5242880 | tf_op jit(solution)/shard_map/all_gather | solution.py:63
  206.2 159.2 %copy-start = (f32[256,2048]{1,0:T(8,128)S(1)}, f32[256,2048]{1,0:T(8,128)}, u32[]{:S(2)}) copy-start(f32[256,2048]{1,0:T(8,128)} %reduce-scatter.6.cloned.1.call-done) | copy-start | bytes 6291460
  450.0 213.9 %reduce-scatter.8.cloned.1.call-start = ((), (), s32[]{:S(2)}) async-start(), calls=%async_computation.10 | async-start | bytes 4325376 | tf_op jit(solution)/shard_map/reduce_scatter | solution.py:67
  495.2 1.6 copy-start.2
Sparse Core Ops, SparseCore 0:
  19.7 171.2 all-gather.2
  495.3 168.5 reduce-scatter.7
Sparse Core Ops, SparseCore 1:
  77.6 96.1 reduce-scatter.5
  205.5 76.4 reduce-scatter.3
  450.1 35.1 all-gather.4
